TPU v7x, 128 devices: a whole 4x4x4 slice. The times are simulated.
128 devices in a mesh: aux: 8 (over z_hi, y), vir: 16 (over z_lo, x, core).
Axes of the slice: x: 4, y: 4, z: 4 (z_hi: 2, z_lo: 2; z = z_hi * 2 + z_lo), core: 2. Of those that a mesh axis runs over, the one named last changes fastest.
Arguments:
- orbitals: bfloat16 [8192, 2, 4096], P('aux', None, 'vir'), may hold values from -0.5390625 to 0.5390625
- screened: bfloat16 [8192, 8192], P('vir', 'aux'), may hold values from -0.0625 to 0.0625
- density_in: float32 [4096, 4096], P('aux', 'vir'), may hold values from -6 to 6
Outputs:
- density: float32 [4096, 4096], P('aux', 'vir')
All inputs are finite; a program needn't handle non-finite values.
Results may differ from a plain program's by a relative error of at most 0.008.
Values may be sent and summed in bfloat16 or wider, within the bound.
No kernel may reach another device: no remote copies, remote signals or barrier semaphores. Data moves between devices by JAX's collectives and lax.ppermute only.
A program may use at most 128 MiB of HBM per device.

v0:
```python
import jax
import jax.numpy as jnp
from jax import lax
from jax.sharding import PartitionSpec as P


def cut_along(x, dim, length):
    before, after = (x.shape[:dim], x.shape[dim + 1 :])
    return jnp.moveaxis(x.reshape(*before, length, -1, *after), dim, 0)


def sum_at_owner(x, axis, dim):
    tiles = cut_along(x, dim, lax.axis_size(axis))
    arrived = lax.all_to_all(tiles, axis, split_axis=0, concat_axis=0, tiled=True)
    return arrived.astype(jnp.float32).sum(axis=0)


def shards(orbitals, screened, density_in):
    row_count, occ_count, col_count = orbitals.shape
    gathered = lax.all_gather(orbitals, "aux", axis=0, tiled=True)
    all_rows = gathered.reshape(gathered.shape[0], occ_count * col_count)
    screened_sum = lax.dot_general(
        lax.all_gather(screened, "vir", axis=0, tiled=True),
        all_rows,
        (((0,), (0,)), ((), ())),
        preferred_element_type=jnp.float32,
    )
    screened_orb = screened_sum.astype(jnp.bfloat16).reshape(row_count * occ_count, col_count)
    all_cols = lax.all_gather(orbitals, "vir", axis=2, tiled=True)
    all_cols = all_cols.reshape(row_count * occ_count, all_cols.shape[2])
    partial_value = lax.dot_general(
        all_cols, screened_orb, (((0,), (0,)), ((), ())), preferred_element_type=jnp.float32
    )
    summed = sum_at_owner(partial_value.astype(jnp.bfloat16), "aux", 0)
    return density_in + summed


def solution(mesh):
    return jax.shard_map(
        shards,
        mesh=mesh,
        in_specs=(P("aux", None, "vir"), P("vir", "aux"), P("aux", "vir")),
        out_specs=P("aux", "vir"),
        check_vma=False,
    )
```

profile of v0, /device:TPU:24, one launch (start us, length us, event | category | flops | bytes accessed | tf_op | source)
XLA Modules:
  0.0 391.0 jit_solution(11248650012446783445)
XLA Ops:
  6.5 0.0 all-gather.6.cloned.1.call-start
  6.5 0.7 all-gather.6.cloned.1.call-update
  7.3 0.0 all-gather.4.cloned.1.call-start
  7.3 0.7 all-gather.4.cloned.1.call-update
  8.0 0.0 all-gather.8.cloned.1.call-start
  8.1 0.7 all-gather.8.cloned.1.call-update
  8.7 109.7 %all-gather.6.cloned.1.call-done = bf16[8192,2,256]{2,1,0:T(2,128)(2,1)} async-done(((bf16[1024,2,256]{2,1,0:T(2,128)(2,1)}), bf16[8192,2,256]{2,1,0:T(2,128)(2,1)}) %all-gather.6.cloned.1.call-update) | async-done | bytes 8388624 | tf_op jit(solution)/shard_map/all_gather | solution.py:20
  118.4 8.0 %copy.10 = bf16[1024,8,2,256]{3,1,2,0:T(8,128)(2,1)} copy(bf16[1024,8,2,256]{3,2,1,0:T(2,128)(2,1)} %bitcast.12) | data formatting | bytes 16777216
  126.4 84.9 %all-gather.4.cloned.1.call-done = bf16[8192,1024]{1,0:T(8,128)(2,1)} async-done(((bf16[512,1024]{1,0:T(8,128)(2,1)}), bf16[8192,1024]{1,0:T(8,128)(2,1)}) %all-gather.4.cloned.1.call-update) | async-done | bytes 16777232 | tf_op jit(solution)/shard_map/all_gather | solution.py:23
  211.3 14.8 %convolution_convert_fusion.1 = bf16[1024,512]{1,0:T(8,128)(2,1)S(1)} fusion(bf16[8192,1024]{1,0:T(8,128)(2,1)} %all-gather.4.cloned.1.call-done, bf16[8192,512]{1,0:T(8,128)(2,1)} %bitcast.13), kind=kOutput, calls=%fused_computation.3 | convolution fusion | flops 8590458880 | bytes 26214400 | tf_op jit(solution)/shard_map/dot_general | solution.py:22
  226.1 0.4 reshape.13
  226.5 85.0 %all-gather.8.cloned.1.call-done = bf16[1024,2,4096]{2,1,0:T(2,128)(2,1)} async-done(((bf16[1024,2,256]{2,1,0:T(2,128)(2,1)}), bf16[1024,2,4096]{2,1,0:T(2,128)(2,1)}) %all-gather.8.cloned.1.call-update) | async-done | bytes 16777232 | tf_op jit(solution)/shard_map/all_gather | solution.py:29
  311.5 24.9 %reshape.14 = bf16[2048,4096]{1,0:T(8,128)(2,1)} reshape(bf16[1024,2,4096]{2,1,0:T(2,128)(2,1)} %all-gather.8.cloned.1.call-done) | data formatting | bytes 33554432 | tf_op jit(solution)/shard_map/reshape | solution.py:30
  336.4 8.4 %convolution_convert_fusion = bf16[256,4096]{1,0:T(8,128)(2,1)S(1)} fusion(bf16[2048,256]{1,0:T(8,128)(2,1)S(1)} %reshape.13, bf16[2048,4096]{1,0:T(8,128)(2,1)} %reshape.14), kind=kOutput, calls=%fused_computation | convolution fusion | flops 4296015872 | bytes 19922944 | tf_op jit(solution)/shard_map/dot_general | solution.py:31
  344.8 0.0 copy-start
  344.9 1.5 copy.12
  346.4 7.1 %all-to-all-start = ((bf16[8,512,256]{1,2,0:T(8,128)(2,1)}), bf16[8,512,256]{1,2,0:T(8,128)(2,1)S(1)}, u32[]{:S(2)}, u32[]{:S(2)}) async-start(bf16[8,512,256]{1,2,0:T(8,128)(2,1)} %bitcast.14), calls=%async_computation | async-start | bytes 4194304 | tf_op jit(solution)/shard_map/all_to_all | solution.py:14
  353.5 0.0 copy-done
  353.5 0.2 copy.6
  353.7 29.4 %all-to-all-done = bf16[8,512,256]{1,2,0:T(8,128)(2,1)S(1)} async-done(((bf16[8,512,256]{1,2,0:T(8,128)(2,1)}), bf16[8,512,256]{1,2,0:T(8,128)(2,1)S(1)}, u32[]{:S(2)}, u32[]{:S(2)}) %all-to-all-start) | async-done | bytes 2097184 | tf_op jit(solution)/shard_map/all_to_all | solution.py:14
  383.1 0.3 convert_reduce_fusion
  383.4 0.1 add.3
  383.5 1.0 copy.7
Async XLA Ops:
  6.5 111.9 %all-gather.6.cloned.1.call-start = ((), (), s32[]{:S(2)}) async-start(), calls=%async_computation.2 | async-start | bytes 9437184 | tf_op jit(solution)/shard_map/all_gather | solution.py:20
  7.3 204.0 %all-gather.4.cloned.1.call-start = ((), (), s32[]{:S(2)}) async-start(), calls=%async_computation.1 | async-start | bytes 17825792 | tf_op jit(solution)/shard_map/all_gather | solution.py:23
  8.0 303.5 %all-gather.8.cloned.1.call-start = ((), (), s32[]{:S(2)}) async-start(), calls=%async_computation.3 | async-start | bytes 17825792 | tf_op jit(solution)/shard_map/all_gather | solution.py:29
  344.8 8.6 %copy-start = (f32[512,256]{1,0:T(8,128)S(1)}, f32[512,256]{1,0:T(8,128)}, u32[]{:S(2)}) copy-start(f32[512,256]{1,0:T(8,128)} %param.5) | copy-start | bytes 1572868
  346.4 36.7 %all-to-all-start = ((bf16[8,512,256]{1,2,0:T(8,128)(2,1)}), bf16[8,512,256]{1,2,0:T(8,128)(2,1)S(1)}, u32[]{:S(2)}, u32[]{:S(2)}) async-start(bf16[8,512,256]{1,2,0:T(8,128)(2,1)} %bitcast.14), calls=%async_computation | async-start | bytes 4194304 | tf_op jit(solution)/shard_map/all_to_all | solution.py:14
Sparse Core Ops, SparseCore 0:
  9.7 108.6 all-gather.5
  120.1 91.1 all-gather.3
  212.9 98.5 all-gather.7
where the time goes:
time: 392 us; the launch traced here: 391 us
  waiting for transfers between devices  311 us (79%)
  local copies, waits for them, and re-layouts  36 us (9%)
  matrix products  23.2 us (6%)
  between operations  13.2 us (3%)
  starting transfers between devices  7.13 us (2%)
    all_gather x1, waiting for transfers between devices, shards(): gathered = lax.all_gather(orbitals, 'aux', axis=0, tiled=True)  110 us
    all_gather x1, waiting for transfers between devices, shards(): all_cols = lax.all_gather(orbitals, 'vir', axis=2, tiled=True)  85 us
    all_gather x1, waiting for transfers between devices, shards(): lax.all_gather(screened, 'vir', axis=0, tiled=True)  84.9 us
    all_to_all x1, waiting for transfers between devices, sum_at_owner(): lax.all_to_all(tiles, axis, split_axis=0, concat_axis=0, tiled=True)  29.4 us
    reshape x1, local copies, waits for them, and re-layouts, shards(): all_cols = all_cols.reshape(row_count * occ_count, all_cols.shape[2])  24.9 us
    dot_general x1, matrix products, shards(): lax.dot_general(lax.all_gather(screened, 'vir', axis=0, tiled=True), all_...  14.8 us
    dot_general x1, matrix products, shards(): lax.dot_general(all_cols, screened_orb, (((0,), (0,)), ((), ())), preferr...  8.43 us
    unnamed x4, local copies, waits for them, and re-layouts  8.21 us
  transfers between devices with their start and end apart: 4, of which 4 were waited for; matrix products, arithmetic and copies ran while one was open for 6% of the time, Pallas kernels for 0%

commit v1 on v0

v1 whole, which is shorter than its diff:
```python
import functools

import jax
import jax.numpy as jnp
from jax import lax
from jax.experimental import pallas as pl
from jax.experimental.pallas import tpu as pltpu
from jax.sharding import Mesh
from jax.sharding import PartitionSpec as P


AXES = ("zh", "y", "zl", "x", "c")
BF = jnp.bfloat16
F32 = jnp.float32
ANY = pl.BlockSpec(memory_space=pl.ANY)
HBM = pl.BlockSpec(memory_space=pltpu.HBM)
VMEM = pl.BlockSpec(memory_space=pltpu.VMEM)
SMEM = pl.BlockSpec(memory_space=pltpu.SMEM)


def flat(x, y, z, c):
    x, y, z = x % 4, y % 4, z % 4
    return ((z // 2) * 4 + y) * 16 + (z % 2) * 8 + x * 2 + c


def table(move):
    pairs = []
    for x in range(4):
        for y in range(4):
            for z in range(4):
                for c in range(2):
                    pairs.append((flat(x, y, z, c), flat(*move(x, y, z, c))))
    return sorted(pairs)


def turn(c):
    return 1 - 2 * c


XF = table(lambda x, y, z, c: (x + turn(c), y, z, c))
XG = table(lambda x, y, z, c: (x - turn(c), y, z, c))
YF = table(lambda x, y, z, c: (x, y + turn(c), z, c))
YG = table(lambda x, y, z, c: (x, y - turn(c), z, c))
ZF = table(lambda x, y, z, c: (x, y, z + turn(c), c))
ZG = table(lambda x, y, z, c: (x, y, z - turn(c), c))
Z2 = table(lambda x, y, z, c: (x, y, z + 2, c))
ZN = table(lambda x, y, z, c: (x, y, z ^ 1, c))
CC = table(lambda x, y, z, c: (x, y, z, 1 - c))
ZNC = table(lambda x, y, z, c: (x, y, z ^ 1, 1 - c))


def send(v, pairs):
    return lax.ppermute(v, AXES, pairs)


def call(kernel, outs, out_specs, in_specs, scratch, flops=0, aliases=None, limit=16):
    return pl.pallas_call(
        kernel,
        out_shape=outs,
        in_specs=in_specs,
        out_specs=out_specs,
        scratch_shapes=scratch,
        input_output_aliases=aliases or {},
        compiler_params=pltpu.CompilerParams(vmem_limit_bytes=limit << 20),
        cost_estimate=pl.CostEstimate(flops=flops, bytes_accessed=4 << 20, transcendentals=0),
    )


def sems(*shape):
    return pltpu.SemaphoreType.DMA(shape)


def run_copies(copies):
    for copy in copies:
        copy.start()
    return copies


def finish_copies(copies):
    for copy in copies:
        copy.wait()


def first_kernel(slots, idx, *refs):
    n = len(slots)
    ws, bs, outs, (wv, bv, ov, wsem, bsem, osem) = refs[:16], refs[16:20], refs[20 : 20 + n], refs[20 + n :]

    def w_copy(at, q, k):
        place = wv.at[at, pl.ds(q // 2 * 256, 256), pl.ds(q % 2 * 1024, 1024)]
        return pltpu.make_async_copy(ws[q * 4 + k], place, wsem.at[at, q])

    def b_place(v):
        return bv.at[v % 2, pl.ds(pl.multiple_of(v // 2 * 1024, 1024), 1024)]

    b_copies = run_copies([pltpu.make_async_copy(bs[k], b_place(idx[4 + k]), bsem.at[k]) for k in range(4)])
    for at, j in enumerate(slots):
        for k in range(4):

            @pl.when(idx[j] == k)
            def _(at=at, k=k):
                run_copies([w_copy(at, q, k) for q in range(4)])

    finish_copies(b_copies)
    writes = []
    for at in range(n):
        finish_copies([w_copy(at, q, 0) for q in range(4)])
        for low in range(2):
            acc = jnp.dot(wv[at], bv[low], preferred_element_type=F32)
            ov[at, :, low * 256 : (low + 1) * 256] = acc.astype(BF)
        writes += run_copies([pltpu.make_async_copy(ov.at[at], outs[at], osem.at[at])])
    finish_copies(writes)


def first_product(slots, idx, ws, bs):
    n = len(slots)
    scratch = [
        pltpu.VMEM((n, 512, 2048), BF),
        pltpu.VMEM((2, 2048, 256), BF),
        pltpu.VMEM((n, 512, 512), BF),
        sems(n, 4),
        sems(4),
        sems(n),
    ]
    return call(
        functools.partial(first_kernel, slots),
        ((pltpu.HBM if n == 4 else jax.ShapeDtypeStruct)((512, 512), BF),) * n,
        (HBM if n == 4 else ANY,) * n,
        [SMEM] + [ANY] * 20,
        scratch,
        flops=n * 2 * 512 * 2048 * 512,
        limit=3 + (5 * n + 1) // 2,
    )(idx, *ws, *bs)


def split_kernel(idx, a, b, c, o0, o1, o2, o3):
    for k, out in enumerate((o0, o1, o2, o3)):
        at = pl.ds(pl.multiple_of(idx[k] * 128, 128), 128)
        total = a[:, at].astype(F32) + b[:, at].astype(F32) + c[:, at].astype(F32)
        out[...] = total.astype(BF)


def split_sum(idx, a, b, c):
    out = jax.ShapeDtypeStruct((a.shape[0], 128), BF)
    return pl.pallas_call(
        split_kernel,
        out_shape=(out,) * 4,
        in_specs=[SMEM] + [VMEM] * 3,
        out_specs=(VMEM,) * 4,
        compiler_params=pltpu.CompilerParams(vmem_limit_bytes=8 << 20),
        cost_estimate=pl.CostEstimate(flops=3 * a.size, bytes_accessed=8 * a.size, transcendentals=0),
        name="split_sum",
    )(idx, a, b, c)


def load_b_kernel(idx, *refs):
    bs, bv, sem = refs[:16], refs[16], refs[17]
    copies = []
    for i in range(2):
        for k in range(8):
            v = idx[k]
            at = pl.ds(pl.multiple_of(i * 2048 + v // 4 * 1024, 1024), 1024)
            copies.append(pltpu.make_async_copy(bs[i * 8 + k], bv.at[v % 4, at], sem.at[i * 8 + k]))
    finish_copies(run_copies(copies))


def load_b(idx, bs):
    return call(
        load_b_kernel, jax.ShapeDtypeStruct((4, 4096, 256), BF), VMEM, [SMEM] + [ANY] * 16, [sems(16)], limit=1
    )(idx, *bs)


def second_kernel(n_ts, idx, bv, *refs):
    ts, refs = refs[: 2 * n_ts], refs[2 * n_ts :]
    if n_ts == 1:
        early, outs, (tv, tt, every, tsem, esem, osem) = refs[0], refs[1:5], refs[5:]
        moves = run_copies(
            [
                pltpu.make_async_copy(early.at[pl.ds(n * 128, 128)], every.at[k], esem.at[n])
                for n, k in enumerate((0, 1, 3))
            ]
        )
    else:
        out, (tv, tt, tsem) = refs[0], refs[1:]
    copies = run_copies([pltpu.make_async_copy(t, tv.at[n], tsem.at[n]) for n, t in enumerate(ts)])
    for n, copy in enumerate(copies):
        copy.wait()
        k, i = n // 2, n % 2
        for rz in range(4):
            for ch in range(2):
                at = pl.ds(pl.multiple_of(i * 2048 + idx[8 + rz * 2 + ch] * 256, 256), 256)
                tt[k * 128 : (k + 1) * 128, at] = tv[n, rz, ch * 256 : (ch + 1) * 256, :].T
    for n in range(4):
        at = slice(n * 256, (n + 1) * 256)
        acc = jnp.dot(tt[...], bv[n], preferred_element_type=F32).astype(BF)
        if n_ts == 1:
            every[2, :, at] = acc
        else:
            out[:, at] = acc
    if n_ts == 1:
        finish_copies(moves)
        finish_copies(
            run_copies([pltpu.make_async_copy(every.at[idx[16 + j]], outs[j], osem.at[j]) for j in range(4)])
        )


def second_product(idx, bv, ts, early=None):
    n = len(ts) // 2
    scratch = [pltpu.VMEM((2 * n, 4, 512, 128), BF), pltpu.VMEM((n * 128, 4096), BF)]
    if early is None:
        outs, specs, more = jax.ShapeDtypeStruct((n * 128, 1024), BF), VMEM, ()
        scratch += [sems(2 * n)]
    else:
        outs, specs, more = (jax.ShapeDtypeStruct((128, 1024), BF),) * 4, (ANY,) * 4, (early,)
        scratch += [pltpu.VMEM((4, 128, 1024), BF), sems(2), sems(3), sems(4)]
    return call(
        functools.partial(second_kernel, n),
        outs,
        specs,
        [SMEM, VMEM] + [ANY] * (2 * n + len(more)),
        scratch,
        flops=2 * n * 128 * 4096 * 1024,
        limit=12,
    )(idx, bv, *ts, *more)


def tail_kernel(idx, a, b, c, o0, o1, o2, o3):
    for k, out in enumerate((o0, o1, o2, o3)):
        at = pl.ds(pl.multiple_of(idx[k] * 256, 256), 256)
        total = a[:, at].astype(F32) + b[:, at].astype(F32) + c[:, at].astype(F32)
        out[...] = total.astype(out.dtype)


def tail_split(idx, a, b, c):
    rows = a.shape[0]
    near = jax.ShapeDtypeStruct((rows, 256), BF)
    return pl.pallas_call(
        tail_kernel,
        out_shape=(jax.ShapeDtypeStruct((rows, 256), F32), near, near, near),
        in_specs=[SMEM] + [VMEM] * 3,
        out_specs=(VMEM,) * 4,
        compiler_params=pltpu.CompilerParams(vmem_limit_bytes=8 << 20),
        name="tail_split",
    )(idx, a, b, c)


def finish_kernel(idx, density, p0, p1, p2, p3, out):
    for k, piece in enumerate((p0, p1, p2, p3)):
        at = pl.ds(pl.multiple_of(idx[k] * 128, 128), 128)
        out[at, :] = density[at, :] + piece[...].astype(F32)


def finish(idx, density, pieces):
    return pl.pallas_call(
        finish_kernel,
        out_shape=jax.ShapeDtypeStruct(density.shape, F32),
        in_specs=[SMEM] + [VMEM] * 5,
        out_specs=VMEM,
        compiler_params=pltpu.CompilerParams(vmem_limit_bytes=8 << 20),
        name="finish",
    )(idx, density, *pieces)


def ints(values):
    return jnp.stack([jnp.asarray(v, jnp.int32) for v in values])


def step(orbitals, screened, density_in):
    zh, y, zl, x, c = (lax.axis_index(name) for name in AXES)
    z = 2 * zh + zl
    s = 1 - 2 * c
    mod4 = lambda v: lax.rem(v + 8, 4)
    z_at = [mod4(z + s * k) for k in range(4)]
    piece = [mod4(j - s * (x - y)) for j in range(4)]
    first_idx = ints(piece + [(v // 2 ^ zh) * 2 + v % 2 for v in z_at])
    split_idx = ints([z, mod4(z + s), mod4(z - s), mod4(z + 2)])
    from_z = [z, mod4(z - s), mod4(z + s), mod4(z + 2)]
    places = [((v % 2) * 2 + core) * 2 + v // 2 for v in from_z for core in (c, 1 - c)]
    b2_slot = [(v // 2) * 4 + (v % 2) * 2 + core for core in (c, 1 - c) for v in z_at]
    second_idx = ints(b2_slot + places + piece)
    tail_idx = ints([zl * 2 + c, (1 - zl) * 2 + c, zl * 2 + 1 - c, (1 - zl) * 2 + 1 - c])
    finish_idx = ints([c * 2 + zl, c * 2 + 1 - zl, (1 - c) * 2 + zl, (1 - c) * 2 + 1 - zl])

    keep = lax.dynamic_slice_in_dim(screened, zh * 256, 256, 0)
    give = lax.dynamic_slice_in_dim(screened, (1 - zh) * 256, 256, 0)
    b = jnp.transpose(orbitals, (1, 0, 2))
    b0, b1 = b[0], b[1]
    other = send(give, Z2)
    wa_f = send(keep, XF)
    wa_g = send(keep, XG)
    b0_f = send(b0, ZF)
    b0_g = send(b0, ZG)
    wa_ff = send(wa_f, XF)
    wb_f = send(other, XF)
    wb_g = send(other, XG)
    b0_ff = send(b0_f, ZF)
    b1_f = send(b1, ZF)
    b1_g = send(b1, ZG)
    wb_ff = send(wb_g, XG)
    b1_ff = send(b1_g, ZG)
    wa = (keep, wa_g, wa_ff, wa_f)
    wb = (other, wb_g, wb_ff, wb_f)
    swap = lambda four: tuple(send(four[k], CC) for k in (0, 3, 2, 1))
    ws = wa + wb + swap(wa) + swap(wb)
    bs = ((b0, b0_g, b0_ff, b0_f), (b1, b1_g, b1_ff, b1_f))

    t2, t1, t3, t0 = [None] * 2, [None] * 2, [None] * 2, [None] * 2
    (t2[0],) = first_product((2,), first_idx, ws, bs[0])
    t1[0], t3[0], t0[0] = first_product((1, 3, 0), first_idx, ws, bs[0])
    t2[1], t1[1], t3[1], t0[1] = first_product((2, 1, 3, 0), first_idx, ws, bs[1])
    gathered = []
    for i in range(2):
        r1 = send(t2[i], YF)
        mid = (t1[i].astype(F32) + r1.astype(F32)).astype(BF)
        r_g = send(t3[i], YG)
        r_f = send(mid, YF)
        t_own, t_f, t_g, t_2 = split_sum(split_idx, t0[i], r_f, r_g)
        t_2 = send(t_2, Z2)
        t_f = send(t_f, ZF)
        t_g = send(t_g, ZG)
        t = jnp.stack([t_own, t_f, t_g, t_2])
        f = send(t, XF)
        g = send(t, XG)
        far = send(f, XF) if i == 0 else send(g, XG)
        gathered.append((t, g, far, f))
    b_all = load_b(second_idx, [v for i in range(2) for v in bs[i] + swap(bs[i])])
    early = second_product(second_idx, b_all, [gathered[i][k] for k in (0, 1, 3) for i in range(2)])
    d0, d1, d2, d3 = second_product(second_idx, b_all, [gathered[i][2] for i in range(2)], early)

    r1 = send(d2, YF)
    r_g = send(d3, YG)
    mid = (d1.astype(F32) + r1.astype(F32)).astype(BF)
    p_own, p_n, p_c, p_nc = tail_split(tail_idx, d0, send(mid, YF), r_g)
    p_nc = send(p_nc, ZNC)
    p_n = send(p_n, ZN)
    p_c = send(p_c, CC)
    return finish(finish_idx, density_in, (p_own, p_n, p_c, p_nc))


def solution(mesh):
    fine = Mesh(mesh.devices.reshape(2, 4, 2, 4, 2), AXES)
    row, col = ("zh", "y"), ("zl", "x", "c")
    return jax.shard_map(
        step,
        mesh=fine,
        in_specs=(P(row, None, col), P(col, row), P(row, col)),
        out_specs=P(row, col),
        check_vma=False,
    )
```

time: 392 us -> 203 us (0.52)
  the two profiles are of different devices: /device:TPU:24 before, /device:TPU:1 now
where the time goes in v1:
time: 203 us; the launch traced here: 201 us
  starting transfers between devices  80.6 us (40%)
  waiting for transfers between devices  43.6 us (21%)
  local copies, waits for them, and re-layouts  40.5 us (20%)
  Pallas kernels  33.8 us (17%)
  other arithmetic  2.31 us (1%)
    ppermute x53, starting transfers between devices, send(): return lax.ppermute(v, AXES, pairs)  80.6 us
    ppermute x53, waiting for transfers between devices, send(): return lax.ppermute(v, AXES, pairs)  43.6 us
    unnamed x103, local copies, waits for them, and re-layouts  39 us
    pallas_call x3, Pallas kernels, first_product(): call(functools.partial(first_kernel, slots), ((pltpu.HBM if n == 4 else j...  17.9 us
    pallas_call x2, Pallas kernels, second_product(): call(functools.partial(second_kernel, n), outs, specs, [SMEM, VMEM] + [AN...  9.25 us
  transfers between devices with their start and end apart: 53, of which 17 were waited for; matrix products, arithmetic and copies ran while one was open for 2% of the time, Pallas kernels for 14%

profile of v1, /device:TPU:1, one launch (start us, length us, event | category | flops | bytes accessed | tf_op | source)
XLA Modules:
  0.0 201.2 jit_solution(13884915534760095747)
XLA Ops:
  0.0 1.3 constant_dynamic-slice_fusion
  1.3 4.5 %collective-permute-start.17 = (bf16[256,1024]{1,0:T(8,128)(2,1)S(1)}, bf16[256,1024]{1,0:T(8,128)(2,1)S(1)}, u32[]{:S(2)}, u32[]{:S(2)}) collective-permute-start(bf16[256,1024]{1,0:T(8,128)(2,1)S(1)} %get-tuple-element.51), channel_id=1, source_target_pairs={{0,64},{1,65},{2,66},{3,67},{4,68},{5,69},{6,70},{7,71},{8,72},{9,... | collective-permute-start | bytes 1572872 | tf_op jit(solution)/shard_map/ppermute | solution.py:53
  5.8 2.5 %collective-permute-start.15 = (bf16[256,1024]{1,0:T(8,128)(2,1)S(1)}, bf16[256,1024]{1,0:T(8,128)(2,1)S(1)}, u32[]{:S(2)}, u32[]{:S(2)}) collective-permute-start(bf16[256,1024]{1,0:T(8,128)(2,1)S(1)} %get-tuple-element.52.refs_0_), channel_id=1, source_target_pairs={{0,2},{1,7},{2,4},{3,1},{4,6},{5,3},{6,0},{7,5},{8,10},{9,15},{10,... | collective-permute-start | bytes 1572872 | tf_op jit(solution)/shard_map/ppermute | solution.py:53
  8.2 1.7 collective-permute-start.21
  10.0 1.4 copy.6
  12.2 5.2 %collective-permute-done.17.refs_4_ = bf16[256,1024]{1,0:T(8,128)(2,1)S(1)} collective-permute-done((bf16[256,1024]{1,0:T(8,128)(2,1)S(1)}, bf16[256,1024]{1,0:T(8,128)(2,1)S(1)}, u32[]{:S(2)}, u32[]{:S(2)}) %collective-permute-start.17) | collective-permute-done | bytes 524320 | tf_op jit(solution)/shard_map/ppermute | solution.py:53
  17.4 2.8 %collective-permute-start.9 = (bf16[1024,256]{1,0:T(8,128)(2,1)S(1)}, bf16[1024,256]{1,0:T(8,128)(2,1)S(1)}, u32[]{:S(2)}, u32[]{:S(2)}) collective-permute-start(bf16[1024,256]{1,0:T(8,128)(2,1)S(1)} %get-tuple-element.53.refs_8_.refs_16_), channel_id=1, source_target_pairs={{0,8},{1,73},{2,10},{3,75},{4,12},{5,77},{6,14},{7,79},{8,64},{9,1... | collective-permute-start | bytes 1572872 | tf_op jit(solution)/shard_map/ppermute | solution.py:53
  20.4 1.6 collective-permute-done.14.refs_1_
  22.8 2.7 %collective-permute-start.16 = (bf16[256,1024]{1,0:T(8,128)(2,1)S(1)}, bf16[256,1024]{1,0:T(8,128)(2,1)}, u32[]{:S(2)}, u32[]{:S(2)}) collective-permute-start(bf16[256,1024]{1,0:T(8,128)(2,1)S(1)} %collective-permute-done.15.refs_3_), channel_id=1, source_target_pairs={{0,2},{1,7},{2,4},{3,1},{4,6},{5,3},{6,0},{7,5},{8,10},{9,15},{10,... | collective-permute-start | bytes 1572872 | tf_op jit(solution)/shard_map/ppermute | solution.py:53
  25.6 3.9 %collective-permute-start.22 = (bf16[256,1024]{1,0:T(8,128)(2,1)S(1)}, bf16[256,1024]{1,0:T(8,128)(2,1)S(1)}, u32[]{:S(2)}, u32[]{:S(2)}) collective-permute-start(bf16[256,1024]{1,0:T(8,128)(2,1)S(1)} %collective-permute-done.15.refs_3_), channel_id=1, source_target_pairs={{0,1},{1,0},{2,3},{3,2},{4,5},{5,4},{6,7},{7,6},{8,9},{9,8},{10,11... | collective-permute-start | bytes 1572872 | tf_op jit(solution)/shard_map/ppermute | solution.py:53
  31.2 2.5 %collective-permute-start.20 = (bf16[256,1024]{1,0:T(8,128)(2,1)S(1)}, bf16[256,1024]{1,0:T(8,128)(2,1)}, u32[]{:S(2)}, u32[]{:S(2)}) collective-permute-start(bf16[256,1024]{1,0:T(8,128)(2,1)S(1)} %collective-permute-done.17.refs_4_), channel_id=1, source_target_pairs={{0,2},{1,7},{2,4},{3,1},{4,6},{5,3},{6,0},{7,5},{8,10},{9,15},{10,... | collective-permute-start | bytes 1572872 | tf_op jit(solution)/shard_map/ppermute | solution.py:53
  33.7 2.3 %collective-permute-done.1.refs_3_.refs_19_ = bf16[1024,256]{1,0:T(8,128)(2,1)S(1)} collective-permute-done((bf16[1024,256]{1,0:T(8,128)(2,1)S(1)}, bf16[1024,256]{1,0:T(8,128)(2,1)S(1)}, u32[]{:S(2)}, u32[]{:S(2)}) %collective-permute-start.1) | collective-permute-done | bytes 524320 | tf_op jit(solution)/shard_map/ppermute | solution.py:53
  36.8 1.3 collective-permute-start.25
  42.9 2.3 %collective-permute-start.28 = (bf16[256,1024]{1,0:T(8,128)(2,1)}, bf16[256,1024]{1,0:T(8,128)(2,1)}, u32[]{:S(2)}, u32[]{:S(2)}) collective-permute-start(bf16[256,1024]{1,0:T(8,128)(2,1)} %collective-permute-done.18.refs_5_), channel_id=1, source_target_pairs={{0,1},{1,0},{2,3},{3,2},{4,5},{5,4},{6,7},{7,6},{8,9},{9,8},{10,11... | collective-permute-start | bytes 1572872 | tf_op jit(solution)/shard_map/ppermute | solution.py:53
  47.3 2.0 collective-permute-done.19.refs_6_
  50.9 2.6 %collective-permute-start.2 = (bf16[1024,256]{1,0:T(8,128)(2,1)S(1)}, bf16[1024,256]{1,0:T(8,128)(2,1)S(1)}, u32[]{:S(2)}, u32[]{:S(2)}) collective-permute-start(bf16[1024,256]{1,0:T(8,128)(2,1)S(1)} %collective-permute-done.1.refs_3_.refs_19_), channel_id=1, source_target_pairs={{0,8},{1,73},{2,10},{3,75},{4,12},{5,77},{6,14},{7,79},{8,64},{9,1... | collective-permute-start | bytes 1572872 | tf_op jit(solution)/shard_map/ppermute | solution.py:53
  63.9 8.3 %shard_map.40 = (bf16[512,512]{1,0:T(8,128)(2,1)}, bf16[512,512]{1,0:T(8,128)(2,1)}, bf16[512,512]{1,0:T(8,128)(2,1)}, bf16[512,512]{1,0:T(8,128)(2,1)}) custom-call(s32[8]{0:T(128)S(1)} %stack.197.idx, bf16[256,1024]{1,0:T(8,128)(2,1)S(1)} %get-tuple-element.52.refs_0_, bf16[256,1024]{1,0:T(8,128)(2,1)S(1)} %copy-done.19, ...), custom_call_target="tpu_custom_call" | custom-call | flops 4294967296 | bytes 4194304 | tf_op jit(solution)/shard_map/pallas_call | solution.py:124
  72.3 2.7 %collective-permute-start.37 = (bf16[512,512]{1,0:T(8,128)(2,1)}, bf16[512,512]{1,0:T(8,128)(2,1)S(1)}, u32[]{:S(2)}, u32[]{:S(2)}) collective-permute-start(bf16[512,512]{1,0:T(8,128)(2,1)} %get-tuple-element.37), channel_id=1, source_target_pairs={{0,16},{1,49},{2,18},{3,51},{4,20},{5,53},{6,22},{7,55},{8,24},{9,... | collective-permute-start | bytes 1572872 | tf_op jit(solution)/shard_map/ppermute | solution.py:53
  76.4 3.6 %shard_map.39 = bf16[512,512]{1,0:T(8,128)(2,1)S(1)} custom-call(s32[8]{0:T(128)S(1)} %stack.197.idx, bf16[256,1024]{1,0:T(8,128)(2,1)S(1)} %get-tuple-element.52.refs_0_, bf16[256,1024]{1,0:T(8,128)(2,1)S(1)} %copy-done.20, bf16[256,1024]{1,0:T(8,128)(2,1)} %collective-permute-done.16.refs_2_, bf16[256,1024]{1,0:T(8,128)(2,1)S(1)} %copy-done.17, ...), custom_call_target="tpu_custom_call" | custom-call | flops 1073741824 | bytes 4194304 | tf_op jit(solution)/shard_map/pallas_call | solution.py:124
  80.1 2.0 %collective-permute-start.29 = (bf16[512,512]{1,0:T(8,128)(2,1)S(1)}, bf16[512,512]{1,0:T(8,128)(2,1)S(1)}, u32[]{:S(2)}, u32[]{:S(2)}) collective-permute-start(bf16[512,512]{1,0:T(8,128)(2,1)S(1)} %shard_map.39), channel_id=1, source_target_pairs={{0,16},{1,49},{2,18},{3,51},{4,20},{5,53},{6,22},{7,55},{8,24},{9,... | collective-permute-start | bytes 1572872 | tf_op jit(solution)/shard_map/ppermute | solution.py:53
  82.1 6.0 %shard_map.38 = (bf16[512,512]{1,0:T(8,128)(2,1)S(1)}, bf16[512,512]{1,0:T(8,128)(2,1)}, bf16[512,512]{1,0:T(8,128)(2,1)S(1)}) custom-call(s32[8]{0:T(128)S(1)} %stack.197.idx, bf16[256,1024]{1,0:T(8,128)(2,1)S(1)} %get-tuple-element.52.refs_0_, bf16[256,1024]{1,0:T(8,128)(2,1)S(1)} %copy-done.20, bf16[256,1024]{1,0:T(8,128)(2,1)} %collective-permute-done.16.refs_2_, ...), custom_call_target="tpu_custom_call" | custom-call | flops 3221225472 | bytes 4194304 | tf_op jit(solution)/shard_map/pallas_call | solution.py:124
  89.2 3.3 %collective-permute-done.29 = bf16[512,512]{1,0:T(8,128)(2,1)S(1)} collective-permute-done((bf16[512,512]{1,0:T(8,128)(2,1)S(1)}, bf16[512,512]{1,0:T(8,128)(2,1)S(1)}, u32[]{:S(2)}, u32[]{:S(2)}) %collective-permute-start.29) | collective-permute-done | bytes 524320 | tf_op jit(solution)/shard_map/ppermute | solution.py:53
  92.6 3.1 %collective-permute-start.38 = (bf16[512,512]{1,0:T(8,128)(2,1)}, bf16[512,512]{1,0:T(8,128)(2,1)S(1)}, u32[]{:S(2)}, u32[]{:S(2)}) collective-permute-start(bf16[512,512]{1,0:T(8,128)(2,1)} %add_convert_fusion), channel_id=1, source_target_pairs={{0,16},{1,49},{2,18},{3,51},{4,20},{5,53},{6,22},{7,55},{8,24},{9,... | collective-permute-start | bytes 1572872 | tf_op jit(solution)/shard_map/ppermute | solution.py:53
  97.5 7.1 %collective-permute-done.38.b = bf16[512,512]{1,0:T(8,128)(2,1)S(1)} collective-permute-done((bf16[512,512]{1,0:T(8,128)(2,1)}, bf16[512,512]{1,0:T(8,128)(2,1)S(1)}, u32[]{:S(2)}, u32[]{:S(2)}) %collective-permute-start.38) | collective-permute-done | bytes 524320 | tf_op jit(solution)/shard_map/ppermute | solution.py:53
  109.3 3.0 %collective-permute-start.40 = (bf16[512,128]{1,0:T(8,128)(2,1)S(1)}, bf16[512,128]{1,0:T(8,128)(2,1)S(1)}, u32[]{:S(2)}, u32[]{:S(2)}) collective-permute-start(bf16[512,128]{1,0:T(8,128)(2,1)S(1)} %get-tuple-element.40), channel_id=1, source_target_pairs={{0,8},{1,73},{2,10},{3,75},{4,12},{5,77},{6,14},{7,79},{8,64},{9,1... | collective-permute-start | bytes 393224 | tf_op jit(solution)/shard_map/ppermute | solution.py:53
  112.3 1.3 collective-permute-start.42
  113.6 6.9 %collective-permute-start.4 = (bf16[1024,256]{1,0:T(8,128)(2,1)S(1)}, bf16[1024,256]{1,0:T(8,128)(2,1)S(1)}, u32[]{:S(2)}, u32[]{:S(2)}) collective-permute-start(bf16[1024,256]{1,0:T(8,128)(2,1)S(1)} %collective-permute-done.1.refs_3_.refs_19_), channel_id=1, source_target_pairs={{0,1},{1,0},{2,3},{3,2},{4,5},{5,4},{6,7},{7,6},{8,9},{9,8},{10,11... | collective-permute-start | bytes 1572872 | tf_op jit(solution)/shard_map/ppermute | solution.py:53
  121.6 1.4 split_sum.2
  123.4 1.2 collective-permute-start.33
  124.6 1.8 collective-permute-start.34
  126.9 6.4 %collective-permute-start.13 = (bf16[1024,256]{1,0:T(8,128)(2,1)}, bf16[1024,256]{1,0:T(8,128)(2,1)S(1)}, u32[]{:S(2)}, u32[]{:S(2)}) collective-permute-start(bf16[1024,256]{1,0:T(8,128)(2,1)} %copy-done.3), channel_id=1, source_target_pairs={{0,1},{1,0},{2,3},{3,2},{4,5},{5,4},{6,7},{7,6},{8,9},{9,8},{10,11... | collective-permute-start | bytes 1572872 | tf_op jit(solution)/shard_map/ppermute | solution.py:53
  135.7 2.7 %collective-permute-start.35 = (bf16[4,512,128]{2,1,0:T(8,128)(2,1)S(1)}, bf16[4,512,128]{2,1,0:T(8,128)(2,1)}, u32[]{:S(2)}, u32[]{:S(2)}) collective-permute-start(bf16[4,512,128]{2,1,0:T(8,128)(2,1)S(1)} %pad_maximum_fusion.refs_0_), channel_id=1, source_target_pairs={{0,2},{1,7},{2,4},{3,1},{4,6},{5,3},{6,0},{7,5},{8,10},{9,15},{10,... | collective-permute-start | bytes 1572872 | tf_op jit(solution)/shard_map/ppermute | solution.py:53
  142.3 6.0 %collective-permute-done.43.refs_3_ = bf16[4,512,128]{2,1,0:T(8,128)(2,1)} collective-permute-done((bf16[4,512,128]{2,1,0:T(8,128)(2,1)S(1)}, bf16[4,512,128]{2,1,0:T(8,128)(2,1)}, u32[]{:S(2)}, u32[]{:S(2)}) %collective-permute-start.43) | collective-permute-done | bytes 524320 | tf_op jit(solution)/shard_map/ppermute | solution.py:53
  148.2 1.5 collective-permute-done.35.refs_4_
  149.7 3.2 %collective-permute-start.36 = (bf16[4,512,128]{2,1,0:T(8,128)(2,1)}, bf16[4,512,128]{2,1,0:T(8,128)(2,1)}, u32[]{:S(2)}, u32[]{:S(2)}) collective-permute-start(bf16[4,512,128]{2,1,0:T(8,128)(2,1)} %collective-permute-done.35.refs_4_), channel_id=1, source_target_pairs={{0,2},{1,7},{2,4},{3,1},{4,6},{5,3},{6,0},{7,5},{8,10},{9,15},{10,... | collective-permute-start | bytes 1572872 | tf_op jit(solution)/shard_map/ppermute | solution.py:53
  162.4 2.4 %shard_map.37.bv = bf16[4,4096,256]{2,1,0:T(8,128)(2,1)S(1)} custom-call(s32[20]{0:T(128)S(1)} %stack.187.idx, bf16[1024,256]{1,0:T(8,128)(2,1)S(1)} %get-tuple-element.54.refs_0_.refs_16_, bf16[1024,256]{1,0:T(8,128)(2,1)S(1)} %collective-permute-done.refs_1_.refs_17_, bf16[1024,256]{1,0:T(8,128)(2,1)S(1)} %collective-permute-done.2.refs_2_.refs_18_, ...), custom_call_target="tpu_custom_call" | custom-call | bytes 4194304 | tf_op jit(solution)/shard_map/pallas_call | solution.py:167
  164.9 5.8 %shard_map.41.refs_2_ = bf16[384,1024]{1,0:T(8,128)(2,1)S(1)} custom-call(s32[20]{0:T(128)S(1)} %stack.187.idx, bf16[4,4096,256]{2,1,0:T(8,128)(2,1)S(1)} %shard_map.37.bv, bf16[4,512,128]{2,1,0:T(8,128)(2,1)S(1)} %pad_maximum_fusion.refs_0_, bf16[4,512,128]{2,1,0:T(8,128)(2,1)S(1)} %pad_maximum_fusion.1.refs_1_, ...), custom_call_target="tpu_custom_call" | custom-call | flops 3221225472 | bytes 4194304 | tf_op jit(solution)/shard_map/pallas_call | solution.py:215
  170.7 1.1 collective-permute-done.36.refs_0_
  171.9 3.4 %shard_map.42 = (bf16[128,1024]{1,0:T(8,128)(2,1)S(1)}, bf16[128,1024]{1,0:T(8,128)(2,1)S(1)}, bf16[128,1024]{1,0:T(8,128)(2,1)S(1)}, bf16[128,1024]{1,0:T(8,128)(2,1)S(1)}) custom-call(s32[20]{0:T(128)S(1)} %stack.187.idx, bf16[4,4096,256]{2,1,0:T(8,128)(2,1)S(1)} %shard_map.37.bv, bf16[4,512,128]{2,1,0:T(8,128)(2,1)} %collective-permute-done.36.refs_0_, ...), custom_call_target="tpu_custom_call" | custom-call | flops 1073741824 | bytes 4194304 | tf_op jit(solution)/shard_map/pallas_call | solution.py:215
  175.3 1.8 collective-permute-start.47
  177.1 5.0 %collective-permute-done.47 = bf16[128,1024]{1,0:T(8,128)(2,1)S(1)} collective-permute-done((bf16[128,1024]{1,0:T(8,128)(2,1)S(1)}, bf16[128,1024]{1,0:T(8,128)(2,1)S(1)}, u32[]{:S(2)}, u32[]{:S(2)}) %collective-permute-start.47) | collective-permute-done | bytes 262176 | tf_op jit(solution)/shard_map/ppermute | solution.py:53
  182.2 1.9 collective-permute-start.48
  184.1 2.1 %collective-permute-done.49.c = bf16[128,1024]{1,0:T(8,128)(2,1)S(1)} collective-permute-done((bf16[128,1024]{1,0:T(8,128)(2,1)S(1)}, bf16[128,1024]{1,0:T(8,128)(2,1)S(1)}, u32[]{:S(2)}, u32[]{:S(2)}) %collective-permute-start.49) | collective-permute-done | bytes 262176 | tf_op jit(solution)/shard_map/ppermute | solution.py:53
  186.2 1.2 collective-permute-done.48.b
  188.2 6.9 %collective-permute-start.51 = (bf16[128,256]{1,0:T(8,128)(2,1)S(1)}, bf16[128,256]{1,0:T(8,128)(2,1)S(1)}, u32[]{:S(2)}, u32[]{:S(2)}) collective-permute-start(bf16[128,256]{1,0:T(8,128)(2,1)S(1)} %get-tuple-element.49), channel_id=1, source_target_pairs={{0,1},{1,0},{2,3},{3,2},{4,5},{5,4},{6,7},{7,6},{8,9},{9,8},{10,11... | collective-permute-start | bytes 196616 | tf_op jit(solution)/shard_map/ppermute | solution.py:53
  195.2 1.5 collective-permute-start.52
  196.8 3.1 %collective-permute-done.52.p3 = bf16[128,256]{1,0:T(8,128)(2,1)S(1)} collective-permute-done((bf16[128,256]{1,0:T(8,128)(2,1)S(1)}, bf16[128,256]{1,0:T(8,128)(2,1)S(1)}, u32[]{:S(2)}, u32[]{:S(2)}) %collective-permute-start.52) | collective-permute-done | bytes 65568 | tf_op jit(solution)/shard_map/ppermute | solution.py:53
  199.9 1.4 finish.1
  (183 shorter events, 50.9 us)
Async XLA Ops:
  1.3 16.2 %collective-permute-start.17 = (bf16[256,1024]{1,0:T(8,128)(2,1)S(1)}, bf16[256,1024]{1,0:T(8,128)(2,1)S(1)}, u32[]{:S(2)}, u32[]{:S(2)}) collective-permute-start(bf16[256,1024]{1,0:T(8,128)(2,1)S(1)} %get-tuple-element.51), channel_id=1, source_target_pairs={{0,64},{1,65},{2,66},{3,67},{4,68},{5,69},{6,70},{7,71},{8,72},{9,... | collective-permute-start | bytes 1572872 | tf_op jit(solution)/shard_map/ppermute | solution.py:53
  5.8 14.5 %collective-permute-start.15 = (bf16[256,1024]{1,0:T(8,128)(2,1)S(1)}, bf16[256,1024]{1,0:T(8,128)(2,1)S(1)}, u32[]{:S(2)}, u32[]{:S(2)}) collective-permute-start(bf16[256,1024]{1,0:T(8,128)(2,1)S(1)} %get-tuple-element.52.refs_0_), channel_id=1, source_target_pairs={{0,2},{1,7},{2,4},{3,1},{4,6},{5,3},{6,0},{7,5},{8,10},{9,15},{10,... | collective-permute-start | bytes 1572872 | tf_op jit(solution)/shard_map/ppermute | solution.py:53
  8.2 13.8 %collective-permute-start.14 = (bf16[256,1024]{1,0:T(8,128)(2,1)S(1)}, bf16[256,1024]{1,0:T(8,128)(2,1)S(1)}, u32[]{:S(2)}, u32[]{:S(2)}) collective-permute-start(bf16[256,1024]{1,0:T(8,128)(2,1)S(1)} %get-tuple-element.52.refs_0_), channel_id=1, source_target_pairs={{0,6},{1,3},{2,0},{3,5},{4,2},{5,7},{6,4},{7,1},{8,14},{9,11},{10,... | collective-permute-start | bytes 1572872 | tf_op jit(solution)/shard_map/ppermute | solution.py:53
  8.2 13.8 %collective-permute-start.21 = (bf16[256,1024]{1,0:T(8,128)(2,1)S(1)}, bf16[256,1024]{1,0:T(8,128)(2,1)S(1)}, u32[]{:S(2)}, u32[]{:S(2)}) collective-permute-start(bf16[256,1024]{1,0:T(8,128)(2,1)S(1)} %get-tuple-element.52.refs_0_), channel_id=1, source_target_pairs={{0,1},{1,0},{2,3},{3,2},{4,5},{5,4},{6,7},{7,6},{8,9},{9,8},{10,11... | collective-permute-start | bytes 1572872 | tf_op jit(solution)/shard_map/ppermute | solution.py:53
  11.4 14.2 %collective-permute-start.7 = (bf16[1024,256]{1,0:T(8,128)(2,1)S(1)}, bf16[1024,256]{1,0:T(8,128)(2,1)S(1)}, u32[]{:S(2)}, u32[]{:S(2)}) collective-permute-start(bf16[1024,256]{1,0:T(8,128)(2,1)S(1)} %get-tuple-element.53.refs_8_.refs_16_), channel_id=1, source_target_pairs={{0,72},{1,9},{2,74},{3,11},{4,76},{5,13},{6,78},{7,15},{8,0},{9,65... | collective-permute-start | bytes 1572872 | tf_op jit(solution)/shard_map/ppermute | solution.py:53
  17.4 12.9 %collective-permute-start.9 = (bf16[1024,256]{1,0:T(8,128)(2,1)S(1)}, bf16[1024,256]{1,0:T(8,128)(2,1)S(1)}, u32[]{:S(2)}, u32[]{:S(2)}) collective-permute-start(bf16[1024,256]{1,0:T(8,128)(2,1)S(1)} %get-tuple-element.53.refs_8_.refs_16_), channel_id=1, source_target_pairs={{0,8},{1,73},{2,10},{3,75},{4,12},{5,77},{6,14},{7,79},{8,64},{9,1... | collective-permute-start | bytes 1572872 | tf_op jit(solution)/shard_map/ppermute | solution.py:53
  20.3 15.7 %collective-permute-start.1 = (bf16[1024,256]{1,0:T(8,128)(2,1)S(1)}, bf16[1024,256]{1,0:T(8,128)(2,1)S(1)}, u32[]{:S(2)}, u32[]{:S(2)}) collective-permute-start(bf16[1024,256]{1,0:T(8,128)(2,1)S(1)} %get-tuple-element.54.refs_0_.refs_16_), channel_id=1, source_target_pairs={{0,8},{1,73},{2,10},{3,75},{4,12},{5,77},{6,14},{7,79},{8,64},{9,1... | collective-permute-start | bytes 1572872 | tf_op jit(solution)/shard_map/ppermute | solution.py:53
  22.0 14.7 %collective-permute-start.18 = (bf16[256,1024]{1,0:T(8,128)(2,1)S(1)}, bf16[256,1024]{1,0:T(8,128)(2,1)}, u32[]{:S(2)}, u32[]{:S(2)}) collective-permute-start(bf16[256,1024]{1,0:T(8,128)(2,1)S(1)} %collective-permute-done.17.refs_4_), channel_id=1, source_target_pairs={{0,6},{1,3},{2,0},{3,5},{4,2},{5,7},{6,4},{7,1},{8,14},{9,11},{10,... | collective-permute-start | bytes 1572872 | tf_op jit(solution)/shard_map/ppermute | solution.py:53
  22.8 16.1 %collective-permute-start.16 = (bf16[256,1024]{1,0:T(8,128)(2,1)S(1)}, bf16[256,1024]{1,0:T(8,128)(2,1)}, u32[]{:S(2)}, u32[]{:S(2)}) collective-permute-start(bf16[256,1024]{1,0:T(8,128)(2,1)S(1)} %collective-permute-done.15.refs_3_), channel_id=1, source_target_pairs={{0,2},{1,7},{2,4},{3,1},{4,6},{5,3},{6,0},{7,5},{8,10},{9,15},{10,... | collective-permute-start | bytes 1572872 | tf_op jit(solution)/shard_map/ppermute | solution.py:53
  25.6 14.3 %collective-permute-start.22 = (bf16[256,1024]{1,0:T(8,128)(2,1)S(1)}, bf16[256,1024]{1,0:T(8,128)(2,1)S(1)}, u32[]{:S(2)}, u32[]{:S(2)}) collective-permute-start(bf16[256,1024]{1,0:T(8,128)(2,1)S(1)} %collective-permute-done.15.refs_3_), channel_id=1, source_target_pairs={{0,1},{1,0},{2,3},{3,2},{4,5},{5,4},{6,7},{7,6},{8,9},{9,8},{10,11... | collective-permute-start | bytes 1572872 | tf_op jit(solution)/shard_map/ppermute | solution.py:53
  31.2 11.7 %collective-permute-start.20 = (bf16[256,1024]{1,0:T(8,128)(2,1)S(1)}, bf16[256,1024]{1,0:T(8,128)(2,1)}, u32[]{:S(2)}, u32[]{:S(2)}) collective-permute-start(bf16[256,1024]{1,0:T(8,128)(2,1)S(1)} %collective-permute-done.17.refs_4_), channel_id=1, source_target_pairs={{0,2},{1,7},{2,4},{3,1},{4,6},{5,3},{6,0},{7,5},{8,10},{9,15},{10,... | collective-permute-start | bytes 1572872 | tf_op jit(solution)/shard_map/ppermute | solution.py:53
  36.0 9.2 %collective-permute-start.24 = (bf16[256,1024]{1,0:T(8,128)(2,1)S(1)}, bf16[256,1024]{1,0:T(8,128)(2,1)S(1)}, u32[]{:S(2)}, u32[]{:S(2)}) collective-permute-start(bf16[256,1024]{1,0:T(8,128)(2,1)S(1)} %collective-permute-done.14.refs_1_), channel_id=1, source_target_pairs={{0,1},{1,0},{2,3},{3,2},{4,5},{5,4},{6,7},{7,6},{8,9},{9,8},{10,11... | collective-permute-start | bytes 1572872 | tf_op jit(solution)/shard_map/ppermute | solution.py:53
  36.8 9.2 %collective-permute-start.25 = (bf16[256,1024]{1,0:T(8,128)(2,1)S(1)}, bf16[256,1024]{1,0:T(8,128)(2,1)S(1)}, u32[]{:S(2)}, u32[]{:S(2)}) collective-permute-start(bf16[256,1024]{1,0:T(8,128)(2,1)S(1)} %collective-permute-done.17.refs_4_), channel_id=1, source_target_pairs={{0,1},{1,0},{2,3},{3,2},{4,5},{5,4},{6,7},{7,6},{8,9},{9,8},{10,11... | collective-permute-start | bytes 1572872 | tf_op jit(solution)/shard_map/ppermute | solution.py:53
  38.9 10.4 %collective-permute-start.19 = (bf16[256,1024]{1,0:T(8,128)(2,1)}, bf16[256,1024]{1,0:T(8,128)(2,1)}, u32[]{:S(2)}, u32[]{:S(2)}) collective-permute-start(bf16[256,1024]{1,0:T(8,128)(2,1)} %collective-permute-done.18.refs_5_), channel_id=1, source_target_pairs={{0,6},{1,3},{2,0},{3,5},{4,2},{5,7},{6,4},{7,1},{8,14},{9,11},{10,... | collective-permute-start | bytes 1572872 | tf_op jit(solution)/shard_map/ppermute | solution.py:53
  40.8 9.2 %collective-permute-start.8 = (bf16[1024,256]{1,0:T(8,128)(2,1)S(1)}, bf16[1024,256]{1,0:T(8,128)(2,1)S(1)}, u32[]{:S(2)}, u32[]{:S(2)}) collective-permute-start(bf16[1024,256]{1,0:T(8,128)(2,1)S(1)} %collective-permute-done.7.refs_9_.refs_17_), channel_id=1, source_target_pairs={{0,72},{1,9},{2,74},{3,11},{4,76},{5,13},{6,78},{7,15},{8,0},{9,65... | collective-permute-start | bytes 1572872 | tf_op jit(solution)/shard_map/ppermute | solution.py:53
  42.9 10.6 %collective-permute-start.28 = (bf16[256,1024]{1,0:T(8,128)(2,1)}, bf16[256,1024]{1,0:T(8,128)(2,1)}, u32[]{:S(2)}, u32[]{:S(2)}) collective-permute-start(bf16[256,1024]{1,0:T(8,128)(2,1)} %collective-permute-done.18.refs_5_), channel_id=1, source_target_pairs={{0,1},{1,0},{2,3},{3,2},{4,5},{5,4},{6,7},{7,6},{8,9},{9,8},{10,11... | collective-permute-start | bytes 1572872 | tf_op jit(solution)/shard_map/ppermute | solution.py:53
  46.8 6.7 %collective-permute-start.26 = (bf16[256,1024]{1,0:T(8,128)(2,1)}, bf16[256,1024]{1,0:T(8,128)(2,1)}, u32[]{:S(2)}, u32[]{:S(2)}) collective-permute-start(bf16[256,1024]{1,0:T(8,128)(2,1)} %collective-permute-done.20.refs_7_), channel_id=1, source_target_pairs={{0,1},{1,0},{2,3},{3,2},{4,5},{5,4},{6,7},{7,6},{8,9},{9,8},{10,11... | collective-permute-start | bytes 1572872 | tf_op jit(solution)/shard_map/ppermute | solution.py:53
  50.8 25.2 %collective-permute-start = (bf16[1024,256]{1,0:T(8,128)(2,1)S(1)}, bf16[1024,256]{1,0:T(8,128)(2,1)S(1)}, u32[]{:S(2)}, u32[]{:S(2)}) collective-permute-start(bf16[1024,256]{1,0:T(8,128)(2,1)S(1)} %get-tuple-element.54.refs_0_.refs_16_), channel_id=1, source_target_pairs={{0,72},{1,9},{2,74},{3,11},{4,76},{5,13},{6,78},{7,15},{8,0},{9,65... | collective-permute-start | bytes 1572872 | tf_op jit(solution)/shard_map/ppermute | solution.py:53
  50.9 25.5 %collective-permute-start.2 = (bf16[1024,256]{1,0:T(8,128)(2,1)S(1)}, bf16[1024,256]{1,0:T(8,128)(2,1)S(1)}, u32[]{:S(2)}, u32[]{:S(2)}) collective-permute-start(bf16[1024,256]{1,0:T(8,128)(2,1)S(1)} %collective-permute-done.1.refs_3_.refs_19_), channel_id=1, source_target_pairs={{0,8},{1,73},{2,10},{3,75},{4,12},{5,77},{6,14},{7,79},{8,64},{9,1... | collective-permute-start | bytes 1572872 | tf_op jit(solution)/shard_map/ppermute | solution.py:53
  72.3 15.9 %collective-permute-start.37 = (bf16[512,512]{1,0:T(8,128)(2,1)}, bf16[512,512]{1,0:T(8,128)(2,1)S(1)}, u32[]{:S(2)}, u32[]{:S(2)}) collective-permute-start(bf16[512,512]{1,0:T(8,128)(2,1)} %get-tuple-element.37), channel_id=1, source_target_pairs={{0,16},{1,49},{2,18},{3,51},{4,20},{5,53},{6,22},{7,55},{8,24},{9,... | collective-permute-start | bytes 1572872 | tf_op jit(solution)/shard_map/ppermute | solution.py:53
  75.0 37.3 %collective-permute-start.3 = (bf16[1024,256]{1,0:T(8,128)(2,1)S(1)}, bf16[1024,256]{1,0:T(8,128)(2,1)}, u32[]{:S(2)}, u32[]{:S(2)}) collective-permute-start(bf16[1024,256]{1,0:T(8,128)(2,1)S(1)} %get-tuple-element.54.refs_0_.refs_16_), channel_id=1, source_target_pairs={{0,1},{1,0},{2,3},{3,2},{4,5},{5,4},{6,7},{7,6},{8,9},{9,8},{10,11... | collective-permute-start | bytes 1572872 | tf_op jit(solution)/shard_map/ppermute | solution.py:53
  75.9 36.3 %collective-permute-start.10 = (bf16[1024,256]{1,0:T(8,128)(2,1)S(1)}, bf16[1024,256]{1,0:T(8,128)(2,1)}, u32[]{:S(2)}, u32[]{:S(2)}) collective-permute-start(bf16[1024,256]{1,0:T(8,128)(2,1)S(1)} %get-tuple-element.53.refs_8_.refs_16_), channel_id=1, source_target_pairs={{0,1},{1,0},{2,3},{3,2},{4,5},{5,4},{6,7},{7,6},{8,9},{9,8},{10,11... | collective-permute-start | bytes 1572872 | tf_op jit(solution)/shard_map/ppermute | solution.py:53
  75.9 20.7 %collective-permute-start.39 = (bf16[512,512]{1,0:T(8,128)(2,1)}, bf16[512,512]{1,0:T(8,128)(2,1)S(1)}, u32[]{:S(2)}, u32[]{:S(2)}) collective-permute-start(bf16[512,512]{1,0:T(8,128)(2,1)} %get-tuple-element.38), channel_id=1, source_target_pairs={{0,48},{1,17},{2,50},{3,19},{4,52},{5,21},{6,54},{7,23},{8,56},{9,... | collective-permute-start | bytes 1572872 | tf_op jit(solution)/shard_map/ppermute | solution.py:53
  80.1 12.5 %collective-permute-start.29 = (bf16[512,512]{1,0:T(8,128)(2,1)S(1)}, bf16[512,512]{1,0:T(8,128)(2,1)S(1)}, u32[]{:S(2)}, u32[]{:S(2)}) collective-permute-start(bf16[512,512]{1,0:T(8,128)(2,1)S(1)} %shard_map.39), channel_id=1, source_target_pairs={{0,16},{1,49},{2,18},{3,51},{4,20},{5,53},{6,22},{7,55},{8,24},{9,... | collective-permute-start | bytes 1572872 | tf_op jit(solution)/shard_map/ppermute | solution.py:53
  88.2 25.4 %collective-permute-start.31 = (bf16[512,512]{1,0:T(8,128)(2,1)}, bf16[512,512]{1,0:T(8,128)(2,1)}, u32[]{:S(2)}, u32[]{:S(2)}) collective-permute-start(bf16[512,512]{1,0:T(8,128)(2,1)} %get-tuple-element.30), channel_id=1, source_target_pairs={{0,48},{1,17},{2,50},{3,19},{4,52},{5,21},{6,54},{7,23},{8,56},{9,... | collective-permute-start | bytes 1572872 | tf_op jit(solution)/shard_map/ppermute | solution.py:53
  92.6 12.0 %collective-permute-start.38 = (bf16[512,512]{1,0:T(8,128)(2,1)}, bf16[512,512]{1,0:T(8,128)(2,1)S(1)}, u32[]{:S(2)}, u32[]{:S(2)}) collective-permute-start(bf16[512,512]{1,0:T(8,128)(2,1)} %add_convert_fusion), channel_id=1, source_target_pairs={{0,16},{1,49},{2,18},{3,51},{4,20},{5,53},{6,22},{7,55},{8,24},{9,... | collective-permute-start | bytes 1572872 | tf_op jit(solution)/shard_map/ppermute | solution.py:53
  97.4 23.1 %collective-permute-start.30 = (bf16[512,512]{1,0:T(8,128)(2,1)}, bf16[512,512]{1,0:T(8,128)(2,1)}, u32[]{:S(2)}, u32[]{:S(2)}) collective-permute-start(bf16[512,512]{1,0:T(8,128)(2,1)} %add_convert_fusion.1), channel_id=1, source_target_pairs={{0,16},{1,49},{2,18},{3,51},{4,20},{5,53},{6,22},{7,55},{8,24},{9,... | collective-permute-start | bytes 1572872 | tf_op jit(solution)/shard_map/ppermute | solution.py:53
  109.3 13.8 %collective-permute-start.40 = (bf16[512,128]{1,0:T(8,128)(2,1)S(1)}, bf16[512,128]{1,0:T(8,128)(2,1)S(1)}, u32[]{:S(2)}, u32[]{:S(2)}) collective-permute-start(bf16[512,128]{1,0:T(8,128)(2,1)S(1)} %get-tuple-element.40), channel_id=1, source_target_pairs={{0,8},{1,73},{2,10},{3,75},{4,12},{5,77},{6,14},{7,79},{8,64},{9,1... | collective-permute-start | bytes 393224 | tf_op jit(solution)/shard_map/ppermute | solution.py:53
  112.3 11.1 %collective-permute-start.41 = (bf16[512,128]{1,0:T(8,128)(2,1)S(1)}, bf16[512,128]{1,0:T(8,128)(2,1)S(1)}, u32[]{:S(2)}, u32[]{:S(2)}) collective-permute-start(bf16[512,128]{1,0:T(8,128)(2,1)S(1)} %get-tuple-element.41), channel_id=1, source_target_pairs={{0,72},{1,9},{2,74},{3,11},{4,76},{5,13},{6,78},{7,15},{8,0},{9,65... | collective-permute-start | bytes 393224 | tf_op jit(solution)/shard_map/ppermute | solution.py:53
  112.3 12.3 %collective-permute-start.42 = (bf16[512,128]{1,0:T(8,128)(2,1)S(1)}, bf16[512,128]{1,0:T(8,128)(2,1)S(1)}, u32[]{:S(2)}, u32[]{:S(2)}) collective-permute-start(bf16[512,128]{1,0:T(8,128)(2,1)S(1)} %get-tuple-element.42), channel_id=1, source_target_pairs={{0,64},{1,65},{2,66},{3,67},{4,68},{5,69},{6,70},{7,71},{8,72},{9,... | collective-permute-start | bytes 393224 | tf_op jit(solution)/shard_map/ppermute | solution.py:53
  113.6 20.5 %collective-permute-start.4 = (bf16[1024,256]{1,0:T(8,128)(2,1)S(1)}, bf16[1024,256]{1,0:T(8,128)(2,1)S(1)}, u32[]{:S(2)}, u32[]{:S(2)}) collective-permute-start(bf16[1024,256]{1,0:T(8,128)(2,1)S(1)} %collective-permute-done.1.refs_3_.refs_19_), channel_id=1, source_target_pairs={{0,1},{1,0},{2,3},{3,2},{4,5},{5,4},{6,7},{7,6},{8,9},{9,8},{10,11... | collective-permute-start | bytes 1572872 | tf_op jit(solution)/shard_map/ppermute | solution.py:53
  120.5 14.3 %collective-permute-start.6 = (bf16[1024,256]{1,0:T(8,128)(2,1)S(1)}, bf16[1024,256]{1,0:T(8,128)(2,1)S(1)}, u32[]{:S(2)}, u32[]{:S(2)}) collective-permute-start(bf16[1024,256]{1,0:T(8,128)(2,1)S(1)} %collective-permute-done.refs_1_.refs_17_), channel_id=1, source_target_pairs={{0,1},{1,0},{2,3},{3,2},{4,5},{5,4},{6,7},{7,6},{8,9},{9,8},{10,11... | collective-permute-start | bytes 1572872 | tf_op jit(solution)/shard_map/ppermute | solution.py:53
  123.4 9.9 %collective-permute-start.33 = (bf16[512,128]{1,0:T(8,128)(2,1)S(1)}, bf16[512,128]{1,0:T(8,128)(2,1)S(1)}, u32[]{:S(2)}, u32[]{:S(2)}) collective-permute-start(bf16[512,128]{1,0:T(8,128)(2,1)S(1)} %get-tuple-element.33), channel_id=1, source_target_pairs={{0,72},{1,9},{2,74},{3,11},{4,76},{5,13},{6,78},{7,15},{8,0},{9,65... | collective-permute-start | bytes 393224 | tf_op jit(solution)/shard_map/ppermute | solution.py:53
  124.6 8.8 %collective-permute-start.34 = (bf16[512,128]{1,0:T(8,128)(2,1)S(1)}, bf16[512,128]{1,0:T(8,128)(2,1)S(1)}, u32[]{:S(2)}, u32[]{:S(2)}) collective-permute-start(bf16[512,128]{1,0:T(8,128)(2,1)S(1)} %get-tuple-element.34), channel_id=1, source_target_pairs={{0,64},{1,65},{2,66},{3,67},{4,68},{5,69},{6,70},{7,71},{8,72},{9,... | collective-permute-start | bytes 393224 | tf_op jit(solution)/shard_map/ppermute | solution.py:53
  126.9 11.4 %collective-permute-start.13 = (bf16[1024,256]{1,0:T(8,128)(2,1)}, bf16[1024,256]{1,0:T(8,128)(2,1)S(1)}, u32[]{:S(2)}, u32[]{:S(2)}) collective-permute-start(bf16[1024,256]{1,0:T(8,128)(2,1)} %copy-done.3), channel_id=1, source_target_pairs={{0,1},{1,0},{2,3},{3,2},{4,5},{5,4},{6,7},{7,6},{8,9},{9,8},{10,11... | collective-permute-start | bytes 1572872 | tf_op jit(solution)/shard_map/ppermute | solution.py:53
  133.4 5.8 %collective-permute-start.11 = (bf16[1024,256]{1,0:T(8,128)(2,1)}, bf16[1024,256]{1,0:T(8,128)(2,1)S(1)}, u32[]{:S(2)}, u32[]{:S(2)}) collective-permute-start(bf16[1024,256]{1,0:T(8,128)(2,1)} %copy-done.6), channel_id=1, source_target_pairs={{0,1},{1,0},{2,3},{3,2},{4,5},{5,4},{6,7},{7,6},{8,9},{9,8},{10,11... | collective-permute-start | bytes 1572872 | tf_op jit(solution)/shard_map/ppermute | solution.py:53
  133.4 7.5 %collective-permute-start.5 = (bf16[1024,256]{1,0:T(8,128)(2,1)S(1)}, bf16[1024,256]{1,0:T(8,128)(2,1)S(1)}, u32[]{:S(2)}, u32[]{:S(2)}) collective-permute-start(bf16[1024,256]{1,0:T(8,128)(2,1)S(1)} %collective-permute-done.2.refs_2_.refs_18_), channel_id=1, source_target_pairs={{0,1},{1,0},{2,3},{3,2},{4,5},{5,4},{6,7},{7,6},{8,9},{9,8},{10,11... | collective-permute-start | bytes 1572872 | tf_op jit(solution)/shard_map/ppermute | solution.py:53
  134.8 13.4 %collective-permute-start.43 = (bf16[4,512,128]{2,1,0:T(8,128)(2,1)S(1)}, bf16[4,512,128]{2,1,0:T(8,128)(2,1)}, u32[]{:S(2)}, u32[]{:S(2)}) collective-permute-start(bf16[4,512,128]{2,1,0:T(8,128)(2,1)S(1)} %pad_maximum_fusion.1.refs_1_), channel_id=1, source_target_pairs={{0,6},{1,3},{2,0},{3,5},{4,2},{5,7},{6,4},{7,1},{8,14},{9,11},{10,... | collective-permute-start | bytes 1572872 | tf_op jit(solution)/shard_map/ppermute | solution.py:53
  135.7 14.0 %collective-permute-start.35 = (bf16[4,512,128]{2,1,0:T(8,128)(2,1)S(1)}, bf16[4,512,128]{2,1,0:T(8,128)(2,1)}, u32[]{:S(2)}, u32[]{:S(2)}) collective-permute-start(bf16[4,512,128]{2,1,0:T(8,128)(2,1)S(1)} %pad_maximum_fusion.refs_0_), channel_id=1, source_target_pairs={{0,2},{1,7},{2,4},{3,1},{4,6},{5,3},{6,0},{7,5},{8,10},{9,15},{10,... | collective-permute-start | bytes 1572872 | tf_op jit(solution)/shard_map/ppermute | solution.py:53
  139.2 13.9 %collective-permute-start.12 = (bf16[1024,256]{1,0:T(8,128)(2,1)}, bf16[1024,256]{1,0:T(8,128)(2,1)}, u32[]{:S(2)}, u32[]{:S(2)}) collective-permute-start(bf16[1024,256]{1,0:T(8,128)(2,1)} %copy-done.9), channel_id=1, source_target_pairs={{0,1},{1,0},{2,3},{3,2},{4,5},{5,4},{6,7},{7,6},{8,9},{9,8},{10,11... | collective-permute-start | bytes 1572872 | tf_op jit(solution)/shard_map/ppermute | solution.py:53
  140.0 24.9 %collective-permute-start.46 = (bf16[4,512,128]{2,1,0:T(8,128)(2,1)S(1)}, bf16[4,512,128]{2,1,0:T(8,128)(2,1)}, u32[]{:S(2)}, u32[]{:S(2)}) collective-permute-start(bf16[4,512,128]{2,1,0:T(8,128)(2,1)S(1)} %pad_maximum_fusion.1.refs_1_), channel_id=1, source_target_pairs={{0,2},{1,7},{2,4},{3,1},{4,6},{5,3},{6,0},{7,5},{8,10},{9,15},{10,... | collective-permute-start | bytes 1572872 | tf_op jit(solution)/shard_map/ppermute | solution.py:53
  141.6 23.2 %collective-permute-start.45 = (bf16[4,512,128]{2,1,0:T(8,128)(2,1)S(1)}, bf16[4,512,128]{2,1,0:T(8,128)(2,1)}, u32[]{:S(2)}, u32[]{:S(2)}) collective-permute-start(bf16[4,512,128]{2,1,0:T(8,128)(2,1)S(1)} %pad_maximum_fusion.refs_0_), channel_id=1, source_target_pairs={{0,6},{1,3},{2,0},{3,5},{4,2},{5,7},{6,4},{7,1},{8,14},{9,11},{10,... | collective-permute-start | bytes 1572872 | tf_op jit(solution)/shard_map/ppermute | solution.py:53
  148.2 22.5 %collective-permute-start.44 = (bf16[4,512,128]{2,1,0:T(8,128)(2,1)}, bf16[4,512,128]{2,1,0:T(8,128)(2,1)}, u32[]{:S(2)}, u32[]{:S(2)}) collective-permute-start(bf16[4,512,128]{2,1,0:T(8,128)(2,1)} %collective-permute-done.43.refs_3_), channel_id=1, source_target_pairs={{0,6},{1,3},{2,0},{3,5},{4,2},{5,7},{6,4},{7,1},{8,14},{9,11},{10,... | collective-permute-start | bytes 1572872 | tf_op jit(solution)/shard_map/ppermute | solution.py:53
  149.7 22.2 %collective-permute-start.36 = (bf16[4,512,128]{2,1,0:T(8,128)(2,1)}, bf16[4,512,128]{2,1,0:T(8,128)(2,1)}, u32[]{:S(2)}, u32[]{:S(2)}) collective-permute-start(bf16[4,512,128]{2,1,0:T(8,128)(2,1)} %collective-permute-done.35.refs_4_), channel_id=1, source_target_pairs={{0,2},{1,7},{2,4},{3,1},{4,6},{5,3},{6,0},{7,5},{8,10},{9,15},{10,... | collective-permute-start | bytes 1572872 | tf_op jit(solution)/shard_map/ppermute | solution.py:53
  175.3 6.8 %collective-permute-start.47 = (bf16[128,1024]{1,0:T(8,128)(2,1)S(1)}, bf16[128,1024]{1,0:T(8,128)(2,1)S(1)}, u32[]{:S(2)}, u32[]{:S(2)}) collective-permute-start(bf16[128,1024]{1,0:T(8,128)(2,1)S(1)} %get-tuple-element.45), channel_id=1, source_target_pairs={{0,16},{1,49},{2,18},{3,51},{4,20},{5,53},{6,22},{7,55},{8,24},{9,... | collective-permute-start | bytes 786440 | tf_op jit(solution)/shard_map/ppermute | solution.py:53
  177.1 9.1 %collective-permute-start.49 = (bf16[128,1024]{1,0:T(8,128)(2,1)S(1)}, bf16[128,1024]{1,0:T(8,128)(2,1)S(1)}, u32[]{:S(2)}, u32[]{:S(2)}) collective-permute-start(bf16[128,1024]{1,0:T(8,128)(2,1)S(1)} %get-tuple-element.46), channel_id=1, source_target_pairs={{0,48},{1,17},{2,50},{3,19},{4,52},{5,21},{6,54},{7,23},{8,56},{9,... | collective-permute-start | bytes 786440 | tf_op jit(solution)/shard_map/ppermute | solution.py:53
  188.1 8.7 %collective-permute-start.50 = (bf16[128,256]{1,0:T(8,128)(2,1)S(1)}, bf16[128,256]{1,0:T(8,128)(2,1)S(1)}, u32[]{:S(2)}, u32[]{:S(2)}) collective-permute-start(bf16[128,256]{1,0:T(8,128)(2,1)S(1)} %get-tuple-element.48), channel_id=1, source_target_pairs={{0,8},{1,9},{2,10},{3,11},{4,12},{5,13},{6,14},{7,15},{8,0},{9,1},... | collective-permute-start | bytes 196616 | tf_op jit(solution)/shard_map/ppermute | solution.py:53
  188.2 8.6 %collective-permute-start.51 = (bf16[128,256]{1,0:T(8,128)(2,1)S(1)}, bf16[128,256]{1,0:T(8,128)(2,1)S(1)}, u32[]{:S(2)}, u32[]{:S(2)}) collective-permute-start(bf16[128,256]{1,0:T(8,128)(2,1)S(1)} %get-tuple-element.49), channel_id=1, source_target_pairs={{0,1},{1,0},{2,3},{3,2},{4,5},{5,4},{6,7},{7,6},{8,9},{9,8},{10,11... | collective-permute-start | bytes 196616 | tf_op jit(solution)/shard_map/ppermute | solution.py:53
  (56 other events, 249.5 us)
